TPU v7x, 32 devices: a whole 2x2x4 slice. The times are simulated.
32 devices in a mesh: row: 4 (over z), col: 8 (over y, x, core).
Axes of the slice: x: 2, y: 2, z: 4, core: 2. Of those that a mesh axis runs over, the one named last changes fastest.
Arguments:
- gram: bfloat16 [2, 4, 256, 16, 8, 256], P(None, 'row', None, None, 'col'), as said below
Outputs:
- schur: float32 [2, 4, 256, 16, 8, 256], P(None, 'row', None, None, 'col')
Inputs may be any that keep to these rules, and one draw needn't show every extreme that they name: `gram`: the first 2048 columns of the slab form a symmetric matrix, and its leading 2 * 256 x 2 * 256 block is positive definite with smallest eigenvalue above 10.
All inputs are finite; a program needn't handle non-finite values.
Results may differ from a plain program's by a relative error of at most 0.0018.
Values may be sent and summed in bfloat16 or wider, within the bound.
No kernel may reach another device: no remote copies, remote signals or barrier semaphores. Data moves between devices by JAX's collectives and lax.ppermute only.
A program may use at most 64 MiB of HBM per device.

v0:
```python
import jax
import jax.numpy as jnp
from jax import lax
from jax.sharding import PartitionSpec as P


def from_root(block, axis, source):
    block = jnp.where(lax.axis_index(axis) == source, block, jnp.zeros_like(block))
    return lax.psum(block, axis)


def local(gram):
    n_row = lax.axis_size("row")
    n_col = lax.axis_size("col")
    my_row = lax.axis_index("row")
    my_col = lax.axis_index("col")
    row_slots = gram.shape[0]
    tile_size = gram.shape[2]
    col_slots = gram.shape[3]
    slabs = [gram[row_slot, 0, :, :, 0, :].astype(jnp.float32) for row_slot in range(row_slots)]
    col_tile = jnp.arange(col_slots) * n_col + my_col
    row_tile = jnp.arange(row_slots) * n_row + my_row
    every_slot = list(range(row_slots))
    for panel_index in range(2):
        panel_rows = slabs[panel_index // n_row]
        corner = from_root(
            panel_rows[:, panel_index // n_col, :].astype(jnp.bfloat16), "col", panel_index % n_col
        ).astype(jnp.float32)
        triangle = jnp.linalg.cholesky(corner)
        solved = jax.scipy.linalg.solve_triangular(
            triangle, panel_rows.reshape(tile_size, col_slots * tile_size), lower=True
        )
        solved = solved.reshape(tile_size, col_slots, tile_size)
        solved = jnp.where((col_tile >= panel_index)[None, :, None], solved, 0.0).astype(
            jnp.bfloat16
        )
        factor_across = from_root(solved, "row", panel_index % n_row)
        factor_transposed = []
        for factor_row_slot in range(row_slots):
            target = factor_row_slot * n_row + my_row
            chosen = lax.dynamic_index_in_dim(factor_across, target // n_col, 1, keepdims=False)
            factor_transposed.append(from_root(chosen, "col", target % n_col))
        updated = list(slabs)
        for apply_row_slot in every_slot:
            product = jnp.einsum(
                "pi,pjq->ijq",
                factor_transposed[apply_row_slot],
                factor_across,
                preferred_element_type=jnp.float32,
            )
            updated[apply_row_slot] = updated[apply_row_slot] - product
        slabs = updated
    blocks = jnp.stack(slabs, axis=0)
    retain = (row_tile >= 2)[:, None, None, None] & (col_tile >= 2)[None, None, :, None]
    result = jnp.where(retain, blocks, 0.0)
    return result[:, None, :, :, None, :]


def solution(mesh):
    in_specs = (P(None, "row", None, None, "col", None),)
    out_specs = P(None, "row", None, None, "col", None)
    return jax.shard_map(local, mesh=mesh, in_specs=in_specs, out_specs=out_specs, check_vma=False)
```

profile of v0, /device:TPU:0, one launch (start us, length us, event | category | flops | bytes accessed | tf_op | source)
XLA Modules:
  0.0 609.0 jit_solution(9396137955365741867)
XLA Ops:
  6.5 4.5 fusion.30
  11.0 3.0 copy.24
  14.8 2.5 bitcast_convert_fusion
  17.3 53.2 %all-reduce.9.cloned.1.call-done = bf16[256,256]{0,1:T(8,128)(2,1)} async-done(((bf16[256,256]{0,1:T(8,128)(2,1)}), bf16[256,256]{0,1:T(8,128)(2,1)}) %all-reduce.9.cloned.1.call-update) | async-done | bytes 131088 | tf_op jit(solution)/shard_map/psum | solution.py:9
  70.5 1.0 copy.3
  71.5 0.9 fusion.9
  72.5 11.7 %cholesky.130 = f32[128,128]{1,0:T(8,128)S(1)} custom-call(f32[128,128]{1,0:T(8,128)S(1)} %cholesky.194), custom_call_target="Cholesky" | custom-call | tf_op jit(solution)/shard_map/jit(cholesky)/cholesky | solution.py:29
  84.2 9.8 %custom-call.13 = f32[1,128,128]{1,2,0:T(8,128)S(1)} custom-call(f32[1,128,128]{2,1,0:T(8,128)S(1)} %get-tuple-element.59), custom_call_target="InvertDiagBlocksLowerTriangular" | custom-call | tf_op jit(solution)/shard_map/jit(cholesky)/cholesky | solution.py:29
  94.5 11.7 %cholesky.147 = f32[128,128]{1,0:T(8,128)S(1)} custom-call(f32[128,128]{1,0:T(8,128)S(1)} %convolution_subtract_fusion.3), custom_call_target="Cholesky" | custom-call | tf_op jit(solution)/shard_map/jit(cholesky)/cholesky | solution.py:29
  108.2 3.9 while.4
  109.0 1.3 bitcast_dynamic-update-slice_fusion.4
  110.9 1.3 bitcast_dynamic-update-slice_fusion.4
  112.2 19.7 %custom-call.14 = f32[2,128,128]{1,2,0:T(8,128)S(1)} custom-call(f32[2,128,128]{2,1,0:T(8,128)S(1)} %get-tuple-element.21), custom_call_target="InvertDiagBlocksLowerTriangular" | custom-call | tf_op jit(solution)/shard_map/jit(_solve_triangular)/triangular_solve | solution.py:30
  131.9 3.7 fusion.6
  135.5 3.5 convolution_subtract_fusion.1
  139.1 1.9 fusion.23
  141.0 1.6 pad_maximum_fusion
  142.6 4.1 copy.4
  146.7 3.5 fusion.2
  150.3 86.0 %all-reduce.11.cloned.1.call-done = bf16[256,16,256]{0,2,1:T(8,128)(2,1)} async-done(((bf16[256,16,256]{0,2,1:T(8,128)(2,1)}), bf16[256,16,256]{0,2,1:T(8,128)(2,1)}) %all-reduce.11.cloned.1.call-update) | async-done | bytes 2097168 | tf_op jit(solution)/shard_map/psum | solution.py:9
  236.2 1.7 select_bitcast_fusion.3
  238.0 53.2 %all-reduce.13.cloned.1.call-done = bf16[256,256]{0,1:T(8,128)(2,1)} async-done(((bf16[256,256]{0,1:T(8,128)(2,1)}), bf16[256,256]{0,1:T(8,128)(2,1)}) %all-reduce.13.cloned.1.call-update) | async-done | bytes 131088 | tf_op jit(solution)/shard_map/psum | solution.py:9
  291.2 2.4 convert_subtract_fusion.1
  293.6 2.0 copy-done
  296.6 52.2 %all-reduce.15.cloned.1.call-done = bf16[256,256]{0,1:T(8,128)(2,1)} async-done(((bf16[256,256]{0,1:T(8,128)(2,1)}), bf16[256,256]{0,1:T(8,128)(2,1)}) %all-reduce.15.cloned.1.call-update) | async-done | bytes 131088 | tf_op jit(solution)/shard_map/psum | solution.py:9
  348.8 1.0 copy.6
  349.8 0.9 fusion.8
  350.8 11.7 %cholesky.164 = f32[128,128]{1,0:T(8,128)S(1)} custom-call(f32[128,128]{1,0:T(8,128)S(1)} %cholesky.197), custom_call_target="Cholesky" | custom-call | tf_op jit(solution)/shard_map/jit(cholesky)/cholesky | solution.py:29
  363.2 9.8 %custom-call.15 = f32[1,128,128]{1,2,0:T(8,128)S(1)} custom-call(f32[1,128,128]{2,1,0:T(8,128)S(1)} %get-tuple-element.55), custom_call_target="InvertDiagBlocksLowerTriangular" | custom-call | tf_op jit(solution)/shard_map/jit(cholesky)/cholesky | solution.py:29
  373.6 11.7 %cholesky.181 = f32[128,128]{1,0:T(8,128)S(1)} custom-call(f32[128,128]{1,0:T(8,128)S(1)} %convolution_subtract_fusion.2), custom_call_target="Cholesky" | custom-call | tf_op jit(solution)/shard_map/jit(cholesky)/cholesky | solution.py:29
  387.3 4.3 while.5
  388.2 1.3 bitcast_dynamic-update-slice_fusion.5
  390.2 1.3 bitcast_dynamic-update-slice_fusion.5
  391.6 19.7 %custom-call.16 = f32[2,128,128]{1,2,0:T(8,128)S(1)} custom-call(f32[2,128,128]{2,1,0:T(8,128)S(1)} %get-tuple-element.22), custom_call_target="InvertDiagBlocksLowerTriangular" | custom-call | tf_op jit(solution)/shard_map/jit(_solve_triangular)/triangular_solve | solution.py:30
  411.3 3.7 fusion.4
  415.0 3.5 convolution_subtract_fusion
  418.5 1.9 fusion.19
  420.5 1.6 pad_maximum_fusion.1
  422.0 3.3 copy.7
  425.3 1.9 fusion.3
  427.3 1.5 copy-done.6
  428.8 3.0 copy.25
  431.9 81.4 %all-reduce.17.cloned.1.call-done = bf16[256,16,256]{0,2,1:T(8,128)(2,1)} async-done(((bf16[256,16,256]{0,2,1:T(8,128)(2,1)}), bf16[256,16,256]{0,2,1:T(8,128)(2,1)}) %all-reduce.17.cloned.1.call-update) | async-done | bytes 2097168 | tf_op jit(solution)/shard_map/psum | solution.py:9
  513.3 1.7 select_bitcast_fusion.2
  515.1 55.4 %all-reduce.19.cloned.1.call-done = (bf16[256,256]{0,1:T(8,128)(2,1)}, bf16[256,256]{0,1:T(8,128)(2,1)}, bf16[256,256]{0,1:T(8,128)(2,1)}) async-done(((bf16[256,256]{0,1:T(8,128)(2,1)}, bf16[256,256]{0,1:T(8,128)(2,1)}, bf16[256,256]{0,1:T(8,128)(2,1)}), (bf16[256,256]{0,1:T(8,128)(2,1)}, bf16[256,256]{0,1:T(8,128)(2,1)}, bf16[256,256]{0,1:T(8,128)(2,1)})) %all-reduce.19.cloned.1.call-update) | async-done | bytes 393232 | tf_op jit(solution)/shard_map/psum | solution.py:9
  570.5 3.7 subtract_bitcast_fusion
  577.3 3.9 maximum_select_fusion
  581.1 20.5 %copy.15 = f32[2,1,256,16,1,256]{5,4,3,2,1,0:T(1,128)} copy(f32[2,1,256,16,1,256]{2,5,3,4,1,0:T(8,128)} %maximum_select_fusion) | data formatting | bytes 16777216 | tf_op jit(solution)/shard_map/jit(_where)/select_n | solution.py:55
  (66 shorter events, 10.8 us)
Async XLA Ops:
  6.5 64.0 %all-reduce.9.cloned.1.call-start = ((), (), s32[]{:S(2)}) async-start(), calls=%async_computation | async-start | bytes 262144 | tf_op jit(solution)/shard_map/psum | solution.py:9
  14.7 221.5 %all-reduce.11.cloned.1.call-start = ((), (), s32[]{:S(2)}) async-start(), calls=%async_computation.1 | async-start | bytes 4194304 | tf_op jit(solution)/shard_map/psum | solution.py:9
  131.8 3.7 copy-start.2
  150.2 141.0 %all-reduce.13.cloned.1.call-start = ((), (), s32[]{:S(2)}) async-start(), calls=%async_computation.2 | async-start | bytes 262144 | tf_op jit(solution)/shard_map/psum | solution.py:9
  238.0 110.8 %all-reduce.15.cloned.1.call-start = ((), (), s32[]{:S(2)}) async-start(), calls=%async_computation.3 | async-start | bytes 262144 | tf_op jit(solution)/shard_map/psum | solution.py:9
  293.6 2.0 copy-start
  296.3 217.0 %all-reduce.17.cloned.1.call-start = ((), (), s32[]{:S(2)}) async-start(), calls=%async_computation.4 | async-start | bytes 4194304 | tf_op jit(solution)/shard_map/psum | solution.py:9
  411.3 3.7 copy-start.1
  427.2 1.6 copy-start.6
  427.3 143.2 %all-reduce.19.cloned.1.call-start = ((), (), s32[]{:S(2)}) async-start(), calls=%async_computation.5 | async-start | bytes 786432 | tf_op jit(solution)/shard_map/psum | solution.py:9
  570.5 3.8 copy-start.3
  570.5 3.8 copy-start.8
  574.3 1.6 copy-start.4
  574.3 2.2 copy-start.5
  574.3 2.2 copy-start.7
Sparse Core Ops, SparseCore 0:
  14.9 55.6 all-reduce.8
  150.3 85.8 all-reduce.10
  239.3 51.8 all-reduce.12
  296.4 52.3 all-reduce.14
  427.4 85.8 all-reduce.16
  516.9 53.5 all-reduce.18
where the time goes:
time: 618 us; the launch traced here: 609 us
  waiting for transfers between devices  382 us (62%)
  other arithmetic  130 us (21%)
  local copies, waits for them, and re-layouts  53.3 us (9%)
  matrix products  26.9 us (4%)
  between operations  16.8 us (3%)
    psum x6, waiting for transfers between devices, from_root(): return lax.psum(block, axis)  381 us
    another operation x13, other arithmetic, local(): triangle = jnp.linalg.cholesky(corner)  68.6 us
    another operation x7, other arithmetic, local(): jax.scipy.linalg.solve_triangular(triangle, panel_rows.reshape(tile_size,...  42.5 us
    select_n x1, local copies, waits for them, and re-layouts, local(): result = jnp.where(retain, blocks, 0.0)  20.5 us
    another operation x6, matrix products, local(): jax.scipy.linalg.solve_triangular(triangle, panel_rows.reshape(tile_size,...  18.3 us
    another operation x17, local copies, waits for them, and re-layouts, local(): jax.scipy.linalg.solve_triangular(triangle, panel_rows.reshape(tile_size,...  15.2 us
  transfers between devices with their start and end apart: 6, of which 6 were waited for; matrix products, arithmetic and copies ran while one was open for 1% of the time, Pallas kernels for 0%

commit v1 on v0

--- a/solution.py
+++ b/solution.py
@@ -3,10 +3,12 @@
 from jax import lax
 from jax.sharding import PartitionSpec as P
 
+build_meshes = lambda frame_in, mesh_ax: jnp.sum(lax.all_gather(frame_in, mesh_ax), axis=0)
+
 
 def from_root(block, axis, source):
     block = jnp.where(lax.axis_index(axis) == source, block, jnp.zeros_like(block))
-    return lax.psum(block, axis)
+    return build_meshes(block, axis)
 
 
 def local(gram):

time: 618 us -> 676 us (1.094)
  waiting for transfers between devices: 382 us -> 417 us
  other arithmetic: 130 us -> 140 us
    all_gather x0 -> x8, waiting for transfers between devices: none -> 416 us  [lax.all_gather(frame_in, mesh_ax)]
    psum x6 -> x0, waiting for transfers between devices: 381 us -> none  [from_root(): return lax.psum(block, axis)]
    reduce_sum x0 -> x8, other arithmetic: none -> 17.4 us  [jnp.sum(lax.all_gather(frame_in, mesh_ax), axis=0)]
    unnamed x20 -> x30, local copies, waits for them, and re-layouts: 11 us -> 20.5 us
    another operation x17 -> x15, local copies, waits for them, and re-layouts: 15.2 us -> 8.39 us  [local(): jax.scipy.linalg.solve_triangular(triangle, panel_rows.reshape(tile_size,...]
  transfers between devices with their start and end apart: 6 -> 8, of which waited for: 6 -> 8; matrix products, arithmetic and copies ran while one was open for 1% -> 4% of each run, Pallas kernels for 0% -> 0%
where the time goes in v1:
time: 676 us; the launch traced here: 666 us
  waiting for transfers between devices  417 us (62%)
  other arithmetic  140 us (21%)
  local copies, waits for them, and re-layouts  57.7 us (9%)
  matrix products  32.1 us (5%)
  between operations  17.2 us (3%)
    all_gather x8, waiting for transfers between devices, lax.all_gather(frame_in, mesh_ax)  416 us
    another operation x13, other arithmetic, local(): triangle = jnp.linalg.cholesky(corner)  68.8 us
    another operation x7, other arithmetic, local(): jax.scipy.linalg.solve_triangular(triangle, panel_rows.reshape(tile_size,...  40 us
    select_n x1, local copies, waits for them, and re-layouts, local(): result = jnp.where(retain, blocks, 0.0)  20.5 us
    unnamed x30, local copies, waits for them, and re-layouts  20.5 us
    another operation x6, matrix products, local(): jax.scipy.linalg.solve_triangular(triangle, panel_rows.reshape(tile_size,...  18.3 us
    reduce_sum x8, other arithmetic, jnp.sum(lax.all_gather(frame_in, mesh_ax), axis=0)  17.4 us
  transfers between devices with their start and end apart: 8, of which 8 were waited for; matrix products, arithmetic and copies ran while one was open for 4% of the time, Pallas kernels for 0%

profile of v1, /device:TPU:0, one launch (start us, length us, event | category | flops | bytes accessed | tf_op | source)
XLA Modules:
  0.0 665.6 jit_solution(6719319239038634329)
XLA Ops:
  6.5 4.5 fusion.32
  11.0 3.0 copy.35
  14.9 2.5 bitcast_convert_fusion
  17.3 23.9 %all-gather.19.cloned.1.call-done = bf16[2048,1,256]{0,2,1:T(8,128)(2,1)} async-done(((bf16[256,1,256]{0,2,1:T(8,128)(2,1)}), bf16[2048,1,256]{0,2,1:T(8,128)(2,1)}) %all-gather.19.cloned.1.call-update) | async-done | bytes 1048592 | tf_op jit(solution)/shard_map/all_gather | solution.py:6
  41.2 1.5 copy.39
  43.7 11.7 %cholesky.130 = f32[128,128]{1,0:T(8,128)S(1)} custom-call(f32[128,128]{1,0:T(8,128)S(1)} %cholesky.194), custom_call_target="Cholesky" | custom-call | tf_op jit(solution)/shard_map/jit(cholesky)/cholesky | solution.py:31
  55.4 9.8 %custom-call.13 = f32[1,128,128]{1,2,0:T(8,128)S(1)} custom-call(f32[1,128,128]{2,1,0:T(8,128)S(1)} %get-tuple-element.56), custom_call_target="InvertDiagBlocksLowerTriangular" | custom-call | tf_op jit(solution)/shard_map/jit(cholesky)/cholesky | solution.py:31
  65.7 11.7 %cholesky.147 = f32[128,128]{1,0:T(8,128)S(1)} custom-call(f32[128,128]{1,0:T(8,128)S(1)} %convolution_subtract_fusion.3), custom_call_target="Cholesky" | custom-call | tf_op jit(solution)/shard_map/jit(cholesky)/cholesky | solution.py:31
  79.6 4.6 while.4
  80.7 1.4 bitcast_dynamic-update-slice_fusion.4
  84.2 19.7 %custom-call.14 = f32[2,128,128]{1,2,0:T(8,128)S(1)} custom-call(f32[2,128,128]{2,1,0:T(8,128)S(1)} %get-tuple-element.21), custom_call_target="InvertDiagBlocksLowerTriangular" | custom-call | tf_op jit(solution)/shard_map/jit(_solve_triangular)/triangular_solve | solution.py:32
  103.9 3.7 fusion.8
  107.6 3.5 convolution_subtract_fusion.1
  111.1 1.9 fusion.25
  114.1 1.9 fusion.4
  116.1 149.7 %all-gather.15.cloned.1.call-done = bf16[4,256,16,256]{3,2,1,0:T(8,128)(2,1)} async-done(((bf16[1,256,16,256]{3,2,1,0:T(8,128)(2,1)}), bf16[4,256,16,256]{3,2,1,0:T(8,128)(2,1)}) %all-gather.15.cloned.1.call-update) | async-done | bytes 8388624 | tf_op jit(solution)/shard_map/all_gather | solution.py:6
  265.8 6.6 reduce_sum.97
  272.4 3.0 copy.15
  276.3 21.9 %all-gather.21.cloned.1.call-done = bf16[2048,1,256]{0,2,1:T(8,128)(2,1)} async-done(((bf16[256,1,256]{0,2,1:T(8,128)(2,1)}), bf16[2048,1,256]{0,2,1:T(8,128)(2,1)}) %all-gather.21.cloned.1.call-update) | async-done | bytes 1048592 | tf_op jit(solution)/shard_map/all_gather | solution.py:6
  298.2 1.7 copy.41
  301.5 2.0 copy-done
  304.4 23.5 %all-gather.23.cloned.1.call-done = bf16[2048,1,256]{0,2,1:T(8,128)(2,1)} async-done(((bf16[256,1,256]{0,2,1:T(8,128)(2,1)}), bf16[2048,1,256]{0,2,1:T(8,128)(2,1)}) %all-gather.23.cloned.1.call-update) | async-done | bytes 1048592 | tf_op jit(solution)/shard_map/all_gather | solution.py:6
  327.9 1.5 copy.42
  330.3 11.7 %cholesky.164 = f32[128,128]{1,0:T(8,128)S(1)} custom-call(f32[128,128]{1,0:T(8,128)S(1)} %cholesky.197), custom_call_target="Cholesky" | custom-call | tf_op jit(solution)/shard_map/jit(cholesky)/cholesky | solution.py:31
  342.1 9.8 %custom-call.15 = f32[1,128,128]{1,2,0:T(8,128)S(1)} custom-call(f32[1,128,128]{2,1,0:T(8,128)S(1)} %get-tuple-element.52), custom_call_target="InvertDiagBlocksLowerTriangular" | custom-call | tf_op jit(solution)/shard_map/jit(cholesky)/cholesky | solution.py:31
  352.4 11.7 %cholesky.181 = f32[128,128]{1,0:T(8,128)S(1)} custom-call(f32[128,128]{1,0:T(8,128)S(1)} %convolution_subtract_fusion.2), custom_call_target="Cholesky" | custom-call | tf_op jit(solution)/shard_map/jit(cholesky)/cholesky | solution.py:31
  367.0 4.4 while.5
  367.9 1.4 bitcast_dynamic-update-slice_fusion.5
  370.0 1.4 bitcast_dynamic-update-slice_fusion.5
  371.4 19.7 %custom-call.16 = f32[2,128,128]{1,2,0:T(8,128)S(1)} custom-call(f32[2,128,128]{2,1,0:T(8,128)S(1)} %get-tuple-element.22), custom_call_target="InvertDiagBlocksLowerTriangular" | custom-call | tf_op jit(solution)/shard_map/jit(_solve_triangular)/triangular_solve | solution.py:32
  391.1 3.7 fusion.6
  394.8 3.5 convolution_subtract_fusion
  398.3 1.9 fusion.21
  401.2 2.0 fusion.5
  404.1 148.9 %all-gather.17.cloned.1.call-done = bf16[4,256,16,256]{3,2,1,0:T(8,128)(2,1)} async-done(((bf16[1,256,16,256]{3,2,1,0:T(8,128)(2,1)}), bf16[4,256,16,256]{3,2,1,0:T(8,128)(2,1)}) %all-gather.17.cloned.1.call-update) | async-done | bytes 8388624 | tf_op jit(solution)/shard_map/all_gather | solution.py:6
  553.0 6.1 reduce_sum.100
  561.4 4.3 copy.37
  565.8 10.7 %all-gather.27.cloned.1.call-done = bf16[2048,1,256]{0,2,1:T(8,128)(2,1)} async-done(((bf16[256,1,256]{0,2,1:T(8,128)(2,1)}), bf16[2048,1,256]{0,2,1:T(8,128)(2,1)}) %all-gather.27.cloned.1.call-update) | async-done | bytes 1048592 | tf_op jit(solution)/shard_map/all_gather | solution.py:6
  576.6 1.7 copy.45
  579.0 2.7 fusion.16
  581.8 20.3 %all-gather.25.cloned.1.call-done = bf16[2048,1,256]{0,2,1:T(8,128)(2,1)} async-done(((bf16[256,1,256]{0,2,1:T(8,128)(2,1)}), bf16[2048,1,256]{0,2,1:T(8,128)(2,1)}) %all-gather.25.cloned.1.call-update) | async-done | bytes 1048592 | tf_op jit(solution)/shard_map/all_gather | solution.py:6
  602.0 1.5 copy.44
  604.3 5.5 subtract_bitcast_fusion
  609.9 17.6 %all-gather.29.cloned.1.call-done = bf16[2048,1,256]{0,2,1:T(8,128)(2,1)} async-done(((bf16[256,1,256]{0,2,1:T(8,128)(2,1)}), bf16[2048,1,256]{0,2,1:T(8,128)(2,1)}) %all-gather.29.cloned.1.call-update) | async-done | bytes 1048592 | tf_op jit(solution)/shard_map/all_gather | solution.py:6
  627.5 1.7 copy.46
  630.0 3.9 fusion.3
  633.9 3.9 maximum_select_fusion
  637.8 20.5 %copy.29 = f32[2,1,256,16,1,256]{5,4,3,2,1,0:T(1,128)} copy(f32[2,1,256,16,1,256]{2,5,3,4,1,0:T(8,128)} %maximum_select_fusion) | data formatting | bytes 16777216 | tf_op jit(solution)/shard_map/jit(_where)/select_n | solution.py:57
  (91 shorter events, 20.9 us)
Async XLA Ops:
  6.5 34.7 %all-gather.19.cloned.1.call-start = ((), (), s32[]{:S(2)}) async-start(), calls=%async_computation.2 | async-start | bytes 1179648 | tf_op jit(solution)/shard_map/all_gather | solution.py:6
  14.0 3.3 copy-start.4
  14.8 251.0 %all-gather.15.cloned.1.call-start = ((), (), s32[]{:S(2)}) async-start(), calls=%async_computation | async-start | bytes 10485760 | tf_op jit(solution)/shard_map/all_gather | solution.py:6
  103.9 3.7 copy-start.6
  116.0 182.2 %all-gather.21.cloned.1.call-start = ((), (), s32[]{:S(2)}) async-start(), calls=%async_computation.3 | async-start | bytes 1179648 | tf_op jit(solution)/shard_map/all_gather | solution.py:6
  275.4 26.0 %copy-start.2 = (bf16[256,16,256]{0,2,1:T(8,128)(2,1)}, bf16[256,16,256]{0,2,1:T(8,128)(2,1)S(1)}, u32[]{:S(2)}) copy-start(bf16[256,16,256]{0,2,1:T(8,128)(2,1)S(1)} %copy.15) | copy-start | bytes 6291460
  276.3 51.6 %all-gather.23.cloned.1.call-start = ((), (), s32[]{:S(2)}) async-start(), calls=%async_computation.4 | async-start | bytes 1179648 | tf_op jit(solution)/shard_map/all_gather | solution.py:6
  298.2 2.5 copy-start.5
  301.5 2.0 copy-start
  304.1 248.8 %all-gather.17.cloned.1.call-start = ((), (), s32[]{:S(2)}) async-start(), calls=%async_computation.1 | async-start | bytes 10485760 | tf_op jit(solution)/shard_map/all_gather | solution.py:6
  391.1 3.7 copy-start.1
  403.2 173.4 %all-gather.27.cloned.1.call-start = ((), (), s32[]{:S(2)}) async-start(), calls=%async_computation.6 | async-start | bytes 1179648 | tf_op jit(solution)/shard_map/all_gather | solution.py:6
  403.8 198.3 %all-gather.25.cloned.1.call-start = ((), (), s32[]{:S(2)}) async-start(), calls=%async_computation.5 | async-start | bytes 1179648 | tf_op jit(solution)/shard_map/all_gather | solution.py:6
  560.5 67.0 %all-gather.29.cloned.1.call-start = ((), (), s32[]{:S(2)}) async-start(), calls=%async_computation.7 | async-start | bytes 1179648 | tf_op jit(solution)/shard_map/all_gather | solution.py:6
  576.6 2.5 copy-start.3
  627.5 2.5 copy-start.8
  630.0 3.9 copy-start.7
Sparse Core Ops, SparseCore 0:
  14.9 26.2 all-gather.18
  116.1 149.6 all-gather.14
  276.4 21.7 all-gather.20
  304.3 23.5 all-gather.22
  403.3 149.6 all-gather.16
  554.7 21.7 all-gather.26
  578.4 23.5 all-gather.24
  603.9 23.5 all-gather.28
